TPU v7x, 1024 devices: a whole 8x8x8 slice. The times are simulated.
1024 devices in a mesh: blk: 64 (over x_lo, z, core), group: 16 (over y, x_hi).
Axes of the slice: x: 8 (x_hi: 2, x_lo: 4; x = x_hi * 4 + x_lo), y: 8, z: 8, core: 2. Of those that a mesh axis runs over, the one named last changes fastest.
Arguments:
- img_feat: bfloat16 [131072, 3072], P(('blk', 'group')), may hold values from -0.375 to 0.375
- head_weight: bfloat16 [3072, 512], replicated, may hold values from -1 to 3
- text_emb: bfloat16 [131072, 512], P(('blk', 'group')), may hold values from -0.375 to 0.375
- natural_exponent_factor: float32 [1], replicated, may hold values from 1.6 to 2
- bias: float32 [1], replicated, may hold values from -3.5 to -2.5
Outputs:
- d_feat: float32 [131072, 3072], P(('blk', 'group'))
- d_text: float32 [131072, 512], P(('blk', 'group'))
All inputs are finite; a program needn't handle non-finite values.
Results may differ from a plain program's by a relative error of at most 0.005.
Values may be sent and summed in bfloat16 or wider, within the bound.
A program may use at most 32 MiB of HBM per device.

v0:
```python
import jax
import jax.numpy as jnp
from jax import lax
from jax.sharding import PartitionSpec as P

STEPS = 2


EPS = 1e-06


def passed_along(block, axis, distance):
    devices = range(lax.axis_size(axis))
    route = [((i - distance) % len(devices), i) for i in devices]
    return lax.ppermute(block, axis, route)


def to_unit(values):
    inverse = lax.rsqrt(jnp.sum(values * values, axis=-1, keepdims=True) + EPS)
    return (values * inverse, inverse)


def unit_back(grad_in, unit_rows, inverse):
    return (grad_in - unit_rows * jnp.sum(unit_rows * grad_in, axis=-1, keepdims=True)) * inverse


def body(img_feat, head_weight, text_emb, natural_exponent_factor, bias):
    similarity_multiplier = jnp.exp(natural_exponent_factor[0])
    partner_offset = bias[0]
    projected = jnp.dot(img_feat, head_weight, preferred_element_type=jnp.float32)
    img_unit, img_inv = to_unit(projected)
    img_low = img_unit.astype(jnp.bfloat16)
    txt_unit, txt_inv = to_unit(text_emb.astype(jnp.float32))
    text_piece = txt_unit.astype(jnp.bfloat16)
    row_count = img_feat.shape[0]
    emb_width = text_emb.shape[1]
    panel_rows = row_count * lax.axis_size("group")
    own_slot = lax.axis_index("group") * row_count
    row_ids = lax.broadcasted_iota(jnp.int32, (row_count, 1), 0)
    contract_last = (((1,), (1,)), ((), ()))
    contract_first = (((0,), (0,)), ((), ()))
    images = lax.all_gather(img_low, "group", axis=0, tiled=True)
    image_ids = lax.broadcasted_iota(jnp.int32, (panel_rows, 1), 0)
    piece_ids = lax.broadcasted_iota(jnp.int32, (1, row_count), 1)
    grad_img = jnp.zeros((row_count, emb_width), jnp.float32)
    grad_txt = jnp.zeros((row_count, emb_width), jnp.float32)
    for loop_step in range(STEPS):
        pos_weight = 1.0 if loop_step == 0 else 0.0
        block_rows = lax.all_gather(text_piece, "group", axis=0, tiled=True)
        block_size = block_rows.shape[0]
        matched_similarity_matrix = (
            similarity_multiplier
            * lax.dot_general(
                img_low, block_rows, contract_last, preferred_element_type=jnp.float32
            )
            + partner_offset
        )
        col_ids = lax.broadcasted_iota(jnp.int32, (1, block_size), 1)
        positive = jnp.where(col_ids == own_slot + row_ids, pos_weight, 0.0)
        weights_low = (jax.nn.sigmoid(matched_similarity_matrix) - positive).astype(jnp.bfloat16)
        round_derivative_part = similarity_multiplier * jnp.dot(
            weights_low, block_rows, preferred_element_type=jnp.float32
        )
        own_rows = text_piece
        grad_img = grad_img + round_derivative_part
        matched_similarity_matrix = (
            similarity_multiplier
            * lax.dot_general(images, own_rows, contract_last, preferred_element_type=jnp.float32)
            + partner_offset
        )
        positive = jnp.where(image_ids == own_slot + piece_ids, pos_weight, 0.0)
        weights_low = (jax.nn.sigmoid(matched_similarity_matrix) - positive).astype(jnp.bfloat16)
        caption_share = similarity_multiplier * lax.dot_general(
            weights_low, images, contract_first, preferred_element_type=jnp.float32
        )
        if loop_step > 0:
            caption_share = passed_along(
                caption_share.astype(jnp.bfloat16), "blk", -loop_step
            ).astype(caption_share.dtype)
        grad_txt = grad_txt + caption_share
        if loop_step + 1 < STEPS:
            text_piece = passed_along(text_piece, "blk", 1)
    img_back = unit_back(grad_img, img_unit, img_inv).astype(jnp.bfloat16)
    d_feat = lax.dot_general(
        img_back, head_weight, contract_last, preferred_element_type=jnp.float32
    )
    d_text = unit_back(grad_txt, txt_unit, txt_inv)
    return (d_feat, d_text)


def solution(mesh):
    return jax.shard_map(
        body,
        mesh=mesh,
        in_specs=(P(("blk", "group"), None), P(), P(("blk", "group"), None), P(), P()),
        out_specs=(P(("blk", "group"), None), P(("blk", "group"), None)),
        check_vma=False,
    )
```

profile of v0, /device:TPU:2, one launch (start us, length us, event | category | flops | bytes accessed | tf_op | source)
XLA Modules:
  0.0 373.6 jit_solution(17039923005125405925)
XLA Ops:
  7.2 0.0 copy-start
  7.2 0.0 all-gather.8.cloned.1.call-start
  7.2 1.8 copy-done
  9.1 1.8 multiply_reduce_fusion.1
  10.9 0.8 multiply_convert_fusion.1
  11.6 0.0 all-gather.8.cloned.1.call-update
  11.7 0.0 all-gather.4.cloned.1.call-start
  11.7 0.1 fusion.53
  11.8 0.8 fusion.49
  12.6 0.0 all-gather.4.cloned.1.call-update
  12.6 0.0 all-gather.6.cloned.1.call-start
  12.7 1.9 collective-permute-start
  14.6 17.8 %collective-permute-done = bf16[128,512]{1,0:T(8,128)(2,1)} collective-permute-done((bf16[128,512]{1,0:T(8,128)(2,1)}, bf16[128,512]{1,0:T(8,128)(2,1)}, u32[]{:S(2)}, u32[]{:S(2)}) %collective-permute-start) | collective-permute-done | bytes 131104 | tf_op jit(solution)/shard_map/ppermute | solution.py:15
  32.3 0.0 all-gather.6.cloned.1.call-update
  33.7 100.3 %all-gather.8.cloned.1.call-done = bf16[2048,512]{1,0:T(8,128)(2,1)} async-done(((bf16[128,512]{1,0:T(8,128)(2,1)}), bf16[2048,512]{1,0:T(8,128)(2,1)}) %all-gather.8.cloned.1.call-update) | async-done | bytes 2097168 | tf_op jit(solution)/shard_map/all_gather | solution.py:42
  134.0 4.2 %fusion.27 = bf16[128,512]{1,0:T(8,128)(2,1)} fusion(bf16[2048,512]{1,0:T(8,128)(2,1)} %all-gather.8.cloned.1.call-done, bf16[128,512]{1,0:T(8,128)(2,1)} %collective-permute-done, f32[]{:T(128)} %bitcast.18, f32[]{:T(128)} %bitcast), kind=kOutput, calls=%fused_computation.34 | convolution fusion | flops 538574848 | bytes 2359304 | tf_op jit(solution)/shard_map/dot_general | solution.py:73
  138.2 1.9 collective-permute-start.1
  140.1 104.4 %all-gather.4.cloned.1.call-done = bf16[2048,512]{1,0:T(8,128)(2,1)} async-done(((bf16[128,512]{1,0:T(8,128)(2,1)}), bf16[2048,512]{1,0:T(8,128)(2,1)}) %all-gather.4.cloned.1.call-update) | async-done | bytes 2097168 | tf_op jit(solution)/shard_map/all_gather | solution.py:49
  244.5 4.1 %fusion.28 = f32[128,512]{1,0:T(8,128)} fusion(bf16[2048,512]{1,0:T(8,128)(2,1)} %all-gather.4.cloned.1.call-done, bf16[128,512]{1,0:T(8,128)(2,1)} %multiply_convert_fusion.1, s32[128]{0:T(128)S(1)} %iota_add_fusion, f32[]{:T(128)} %bitcast.16, f32[]{:T(128)} %bitcast), kind=kOutput, calls=%fused_computation.35 | convolution fusion | flops 539230208 | bytes 2490888 | tf_op jit(solution)/shard_map/dot_general | solution.py:61
  248.6 105.8 %all-gather.6.cloned.1.call-done = bf16[2048,512]{1,0:T(8,128)(2,1)} async-done(((bf16[128,512]{1,0:T(8,128)(2,1)}), bf16[2048,512]{1,0:T(8,128)(2,1)}) %all-gather.6.cloned.1.call-update) | async-done | bytes 2097168 | tf_op jit(solution)/shard_map/all_gather | solution.py:49
  354.4 4.1 %multiply_reduce_fusion = (f32[128]{0:T(128)S(1)}, f32[128,512]{1,0:T(8,128)}) fusion(f32[128,512]{1,0:T(8,128)S(1)} %get-tuple-element.3, f32[128]{0:T(128)S(1)} %add_rsqrt_fusion.1, f32[]{:T(128)} %bitcast, f32[128,512]{1,0:T(8,128)} %fusion.28, bf16[2048,512]{1,0:T(8,128)(2,1)} %all-gather.6.cloned.1.call-done, ...), kind=kOutput, calls=%fused_computation.67 | convolution fusion | flops 538771328 | bytes 3015688 | tf_op jit(solution)/shard_map/dot_general | solution.py:61
  358.5 3.3 fusion.54
  361.8 3.6 fusion.50
  365.4 1.7 fusion.52
  (6 shorter events, 0.0 us)
Async XLA Ops:
  7.2 1.9 copy-start
  7.2 4.5 %copy-start.1 = (bf16[128,512]{1,0:T(8,128)(2,1)S(1)}, bf16[128,512]{1,0:T(8,128)(2,1)}, u32[]{:S(2)}) copy-start(bf16[128,512]{1,0:T(8,128)(2,1)} %param.7) | copy-start | bytes 393220
  7.2 126.9 %all-gather.8.cloned.1.call-start = ((), (), s32[]{:S(2)}) async-start(), calls=%async_computation.2 | async-start | bytes 2228224 | tf_op jit(solution)/shard_map/all_gather | solution.py:42
  11.7 232.9 %all-gather.4.cloned.1.call-start = ((), (), s32[]{:S(2)}) async-start(), calls=%async_computation | async-start | bytes 2228224 | tf_op jit(solution)/shard_map/all_gather | solution.py:49
  12.6 341.8 %all-gather.6.cloned.1.call-start = ((), (), s32[]{:S(2)}) async-start(), calls=%async_computation.1 | async-start | bytes 2228224 | tf_op jit(solution)/shard_map/all_gather | solution.py:49
  12.7 19.7 %collective-permute-start = (bf16[128,512]{1,0:T(8,128)(2,1)}, bf16[128,512]{1,0:T(8,128)(2,1)}, u32[]{:S(2)}, u32[]{:S(2)}) collective-permute-start(bf16[128,512]{1,0:T(8,128)(2,1)} %fusion.49), channel_id=1, source_target_pairs={{1008,0},{0,16},{16,32},{32,48},{48,64},{64,80},{80,96},{96,112},{... | collective-permute-start | bytes 393224 | tf_op jit(solution)/shard_map/ppermute | solution.py:15
  138.2 223.6 %collective-permute-start.1 = (bf16[128,512]{1,0:T(8,128)(2,1)}, bf16[128,512]{1,0:T(8,128)(2,1)}, u32[]{:S(2)}, u32[]{:S(2)}) collective-permute-start(bf16[128,512]{1,0:T(8,128)(2,1)} %fusion.27), channel_id=1, source_target_pairs={{16,0},{32,16},{48,32},{64,48},{80,64},{96,80},{112,96},{128,112},... | collective-permute-start | bytes 393224 | tf_op jit(solution)/shard_map/ppermute | solution.py:15
Sparse Core Ops, SparseCore 0:
  12.9 121.0 all-gather.7
  138.9 105.5 all-gather.3
  248.9 105.5 all-gather.5
where the time goes:
time: 374 us
  waiting for transfers between devices  328 us (88%)
  matrix products  21 us (6%)
  between operations  15.1 us (4%)
  starting transfers between devices  3.95 us (1%)
    all_gather x2, waiting for transfers between devices, body(): block_rows = lax.all_gather(text_piece, 'group', axis=0, tiled=True)  210 us
    all_gather x1, waiting for transfers between devices, body(): images = lax.all_gather(img_low, 'group', axis=0, tiled=True)  100 us
    ppermute x2, waiting for transfers between devices, passed_along(): return lax.ppermute(block, axis, route)  17.8 us
    dot_general x2, matrix products, body(): jnp.dot(weights_low, block_rows, preferred_element_type=jnp.float32)  8.17 us
    dot_general x2, matrix products, body(): lax.dot_general(weights_low, images, contract_first, preferred_element_ty...  7.75 us
  transfers between devices with their start and end apart: 5, of which 4 were waited for; matrix products, arithmetic and copies ran while one was open for 4% of the time, Pallas kernels for 0%

commit v1 on v0

v1 whole, which is shorter than its diff:
```python
import functools

import jax
import jax.numpy as jnp
from jax import lax
from jax.experimental import pallas as pl
from jax.experimental.pallas import tpu as pltpu
from jax.sharding import PartitionSpec as P

EPS = 1e-06
MESH = pl.DeviceIdType.MESH
N_Y = 8
N_BLK = 64
ROWS = 128
HALF = 64
EMB = 512
WIDTH = 3072
K_CHUNKS = 4
LAST = (((1,), (1,)), ((), ()))

NEAR = {7: 0, 1: 1, 6: 2, 2: 3, 5: 4, 3: 5, 4: 6, 0: 7}
FAR = {0: 8, 4: 9, 7: 10, 1: 11, 6: 12, 2: 13, 5: 14, 3: 15}


def rows_of(place, half=None):
    if half is None:
        return pl.ds(place * ROWS, ROWS)
    return pl.ds(place * ROWS + half * HALF, HALF)


def kernel(
    nef_ref, bias_ref, txt_ref, feat_hbm, head_hbm, back_ref, dtext_ref,
    feat, head, txts, imgs, img_unit, own_acc, swap_acc, txt_acc,
    swap_out, swap_in, txt_out, txt_in, load_sem, send_sem, recv_sem,
):
    group = lax.axis_index("group")
    blk = lax.axis_index("blk")
    y, xh = group // 2, lax.rem(group, 2)
    up = {"group": lax.rem(y + 1, N_Y) * 2 + xh, "blk": blk}
    down = {"group": lax.rem(y + N_Y - 1, N_Y) * 2 + xh, "blk": blk}
    across = {"group": y * 2 + (1 - xh), "blk": blk}
    flip_next = jnp.where(blk == N_BLK - 1, 1 - xh, xh)
    flip_prev = jnp.where(blk == 0, 1 - xh, xh)
    after = {"group": y * 2 + flip_next, "blk": lax.rem(blk + 1, N_BLK)}
    before = {"group": y * 2 + flip_prev, "blk": lax.rem(blk + N_BLK - 1, N_BLK)}

    barrier = pltpu.get_barrier_semaphore()
    for peer in (up, down, across, after, before):
        pl.semaphore_signal(barrier, inc=1, device_id=peer, device_id_type=MESH)

    depth = WIDTH // K_CHUNKS
    loads = []
    for k in range(K_CHUNKS):
        span = pl.ds(k * depth, depth)
        pair = (
            pltpu.make_async_copy(feat_hbm.at[:, span], feat.at[:, span], load_sem.at[2 * k]),
            pltpu.make_async_copy(head_hbm.at[span], head.at[span], load_sem.at[2 * k + 1]),
        )
        for copy in pair:
            copy.start()
        loads.append(pair)

    copies = []

    def send(src, dst, peer):
        i = len(copies)
        copy = pltpu.make_async_remote_copy(
            src_ref=src, dst_ref=dst, send_sem=send_sem.at[i], recv_sem=recv_sem.at[i],
            device_id=peer, device_id_type=MESH,
        )
        copy.start()
        copies.append(copy)
        return copy

    def ring_hop(buf, places, moved, step, halves=(0, 1)):
        for half in halves:
            for way, peer in ((-1, up), (1, down)):
                src = (way * step) % N_Y
                dst = (way * (step + 1)) % N_Y
                if step == 3 and half != (0 if way == -1 else 1):
                    continue
                if step:
                    moved[src, half].wait_recv()
                moved[dst, half] = send(
                    buf.at[rows_of(places[src], half)], buf.at[rows_of(places[dst], half)], peer
                )
        if step == 3:
            moved[5, 1].wait_recv()
            moved[3, 0].wait_recv()

    def hand_on(slot):
        handed[slot] = send(txts.at[rows_of(NEAR[slot])], txts.at[rows_of(FAR[slot])], after)

    txt_moved, img_moved, swp_moved, handed = {}, {}, {}, {}

    words = txt_ref[...].astype(jnp.float32)
    txt_inv = lax.rsqrt(jnp.sum(words * words, axis=-1, keepdims=True) + EPS)
    txts[rows_of(NEAR[0])] = (words * txt_inv).astype(jnp.bfloat16)

    scale = jnp.exp(jnp.full((1, 1), nef_ref[0], jnp.float32))
    half_scale = 0.5 * scale
    half_bias = 0.5 * bias_ref[0]

    pl.semaphore_wait(barrier, 5)
    ring_hop(txts, NEAR, txt_moved, 0)
    hand_on(0)

    projected = jnp.zeros((ROWS, EMB), jnp.float32)
    for k in range(K_CHUNKS):
        span = pl.ds(k * depth, depth)
        for copy in loads[k]:
            copy.wait()
        projected += jnp.dot(feat[:, span], head[span], preferred_element_type=jnp.float32)
    img_inv = lax.rsqrt(jnp.sum(projected * projected, axis=-1, keepdims=True) + EPS)
    unit = projected * img_inv
    img_unit[...] = unit
    imgs[rows_of(NEAR[0])] = unit.astype(jnp.bfloat16)

    swapped = send(imgs.at[rows_of(NEAR[0])], imgs.at[rows_of(FAR[0])], across)
    ring_hop(imgs, NEAR, img_moved, 0)

    def terms(left, buf, place, pieces, own=False):
        right = buf[pl.ds(place * ROWS, pieces * ROWS)]
        dots = lax.dot_general(left, right, LAST, preferred_element_type=jnp.float32)
        weight = 0.5 * jnp.tanh(half_scale * dots + half_bias) + 0.5
        if own:
            row = lax.broadcasted_iota(jnp.int32, weight.shape, 0)
            col = lax.broadcasted_iota(jnp.int32, weight.shape, 1)
            weight = jnp.where(col == row + (pieces - 1) * ROWS, weight - 1.0, weight)
        return jnp.dot(weight.astype(jnp.bfloat16), right, preferred_element_type=jnp.float32)

    def own_img():
        return imgs[rows_of(NEAR[0])]

    def both_imgs():
        return imgs[pl.ds(NEAR[0] * ROWS, 2 * ROWS)]

    def both_txts():
        return txts[pl.ds(NEAR[0] * ROWS, 2 * ROWS)]

    ring_hop(txts, NEAR, txt_moved, 1)
    hand_on(7)
    hand_on(1)
    own_acc[...] = terms(own_img(), txts, 0, 2)
    ring_hop(imgs, NEAR, img_moved, 1)
    ring_hop(txts, NEAR, txt_moved, 2)
    hand_on(6)
    hand_on(2)
    handed[0].wait_recv()
    txt_acc[...] = terms(both_txts(), imgs, 0, 2)
    own_acc[...] += terms(own_img(), txts, 2, 2)
    ring_hop(txts, NEAR, txt_moved, 3)
    hand_on(5)
    hand_on(3)
    own_acc[...] += terms(own_img(), txts, 4, 2)
    ring_hop(imgs, NEAR, img_moved, 2)
    txt_acc[...] += terms(both_txts(), imgs, 2, 2)
    txt_moved[4, 0].wait_recv()
    txt_moved[4, 1].wait_recv()
    hand_on(4)
    own_acc[...] += terms(own_img(), txts, 6, 2, own=True)

    swapped.wait_recv()
    ring_hop(imgs, FAR, swp_moved, 0)
    swap_img = imgs[rows_of(FAR[0])]
    swap_acc[...] = terms(swap_img, txts, 0, 4)
    swap_acc[...] += terms(swap_img, txts, 4, 4)
    ring_hop(imgs, NEAR, img_moved, 3)
    for a, b in ((0, 4), (7, 1), (6, 2), (5, 3)):
        handed[a].wait_recv() if a else None
        handed[b].wait_recv()
        both = terms(both_imgs(), txts, FAR[a], 2)
        own_acc[...] += both[:ROWS]
        swap_acc[...] += both[ROWS:]
    swap_out[...] = swap_acc[...].astype(jnp.bfloat16)
    returned = send(swap_out, swap_in, across)

    ring_hop(imgs, FAR, swp_moved, 1)
    txt_acc[...] += terms(both_txts(), imgs, 4, 2)
    img_moved[4, 0].wait_recv()
    img_moved[4, 1].wait_recv()
    txt_acc[...] += terms(both_txts(), imgs, 6, 2, own=True)
    txt_acc[...] += terms(both_txts(), imgs, 10, 2)
    ring_hop(imgs, FAR, swp_moved, 2)
    txt_acc[...] += terms(both_txts(), imgs, 12, 2)
    ring_hop(imgs, FAR, swp_moved, 3)
    txt_acc[...] += terms(both_txts(), imgs, 14, 2)
    swp_moved[4, 0].wait_recv()
    swp_moved[4, 1].wait_recv()
    txt_acc[...] += terms(both_txts(), imgs, 8, 2)
    txt_out[...] = txt_acc[ROWS:].astype(jnp.bfloat16)
    given = send(txt_out, txt_in, before)

    def back(grad, unit_rows, inverse):
        return (grad - unit_rows * jnp.sum(unit_rows * grad, axis=-1, keepdims=True)) * inverse

    returned.wait_recv()
    grad = scale * (own_acc[...] + swap_in[...].astype(jnp.float32))
    back_ref[...] = back(grad, img_unit[...], img_inv).astype(jnp.bfloat16)
    given.wait_recv()
    grad = scale * (txt_acc[:ROWS] + txt_in[...].astype(jnp.float32))
    words = txt_ref[...].astype(jnp.float32)
    dtext_ref[...] = back(grad, words * txt_inv, txt_inv)

    for copy in copies:
        copy.wait_send()


N_COPIES = 3 * 14 + 8 + 3


def body(img_feat, head_weight, text_emb, natural_exponent_factor, bias):
    smem = pl.BlockSpec(memory_space=pltpu.SMEM)
    vmem = pl.BlockSpec(memory_space=pltpu.VMEM)
    hbm = pl.BlockSpec(memory_space=pl.ANY)
    back, d_text = pl.pallas_call(
        kernel,
        out_shape=(
            jax.ShapeDtypeStruct((ROWS, EMB), jnp.bfloat16),
            jax.ShapeDtypeStruct((ROWS, EMB), jnp.float32),
        ),
        in_specs=[smem, smem, vmem, hbm, hbm],
        out_specs=(vmem, vmem),
        scratch_shapes=[
            pltpu.VMEM((ROWS, WIDTH), jnp.bfloat16),
            pltpu.VMEM((WIDTH, EMB), jnp.bfloat16),
            pltpu.VMEM((16 * ROWS, EMB), jnp.bfloat16),
            pltpu.VMEM((16 * ROWS, EMB), jnp.bfloat16),
            pltpu.VMEM((ROWS, EMB), jnp.float32),
            pltpu.VMEM((ROWS, EMB), jnp.float32),
            pltpu.VMEM((ROWS, EMB), jnp.float32),
            pltpu.VMEM((2 * ROWS, EMB), jnp.float32),
            pltpu.VMEM((ROWS, EMB), jnp.bfloat16),
            pltpu.VMEM((ROWS, EMB), jnp.bfloat16),
            pltpu.VMEM((ROWS, EMB), jnp.bfloat16),
            pltpu.VMEM((ROWS, EMB), jnp.bfloat16),
            pltpu.SemaphoreType.DMA((2 * K_CHUNKS,)),
            pltpu.SemaphoreType.DMA((N_COPIES,)),
            pltpu.SemaphoreType.DMA((N_COPIES,)),
        ],
        compiler_params=pltpu.CompilerParams(collective_id=0, has_side_effects=True, vmem_limit_bytes=40 * 2**20),
        name="contrast",
    )(natural_exponent_factor, bias, text_emb, img_feat, head_weight)
    d_feat = lax.dot_general(back, head_weight, LAST, preferred_element_type=jnp.float32)
    return (d_feat, d_text)


def solution(mesh):
    return jax.shard_map(
        body,
        mesh=mesh,
        in_specs=(P(("blk", "group"), None), P(), P(("blk", "group"), None), P(), P()),
        out_specs=(P(("blk", "group"), None), P(("blk", "group"), None)),
        check_vma=False,
    )
```

time: 374 us -> 70.2 us (0.19)
  waiting for transfers between devices: 328 us -> 0 us
  Pallas kernels: 0 us -> 61.1 us
  matrix products: 21 us -> 2.29 us
  between operations: 15.1 us -> 1.94 us
  starting transfers between devices: 3.95 us -> 0 us
    all_gather x3 -> x0, waiting for transfers between devices: 311 us -> none  [the longest x2 210 us: body(): block_rows = lax.all_gather(text_piece, 'group', axis=0, tiled=True)]
    pallas_call x0 -> x1, Pallas kernels: none -> 61.1 us  [body(): pl.pallas_call(kernel, out_shape=(jax.ShapeDtypeStruct((ROWS, EMB), jnp.b...]
    dot_general x6 -> x1, matrix products: 21 us -> 2.29 us  [body(): lax.dot_general(back, head_weight, LAST, preferred_element_type=jnp.float32)]
    ppermute x2 -> x0, waiting for transfers between devices: 17.8 us -> none  [passed_along(): return lax.ppermute(block, axis, route)]
    ppermute x2 -> x0, starting transfers between devices: 3.83 us -> none  [passed_along(): return lax.ppermute(block, axis, route)]
  transfers between devices with their start and end apart: 5 -> 0, of which waited for: 4 -> 0; matrix products, arithmetic and copies ran while one was open for 4% -> 0% of each run, Pallas kernels for 0% -> 0%
where the time goes in v1:
time: 70.2 us; the launch traced here: 69.9 us
  Pallas kernels  61.1 us (87%)
  local copies, waits for them, and re-layouts  4.62 us (7%)
  matrix products  2.29 us (3%)
  between operations  1.94 us (3%)
    pallas_call x1, Pallas kernels, body(): pl.pallas_call(kernel, out_shape=(jax.ShapeDtypeStruct((ROWS, EMB), jnp.b...  61.1 us
    unnamed x7, local copies, waits for them, and re-layouts  4.62 us
    dot_general x1, matrix products, body(): lax.dot_general(back, head_weight, LAST, preferred_element_type=jnp.float32)  2.29 us

profile of v1, /device:TPU:2, one launch (start us, length us, event | category | flops | bytes accessed | tf_op | source)
XLA Modules:
  0.0 69.9 jit_solution(1173845801989622034)
XLA Ops:
  1.9 0.0 copy-start
  1.9 1.9 %copy-done = bf16[3072,512]{1,0:T(8,128)(2,1)S(1)} copy-done((bf16[3072,512]{1,0:T(8,128)(2,1)S(1)}, bf16[3072,512]{1,0:T(8,128)(2,1)}, u32[]{:S(2)}) %copy-start) | copy-done | bytes 3145752
  3.8 0.0 copy-start.1
  3.8 1.1 %copy-done.1 = bf16[128,3072]{1,0:T(8,128)(2,1)S(1)} copy-done((bf16[128,3072]{1,0:T(8,128)(2,1)S(1)}, bf16[128,3072]{1,0:T(8,128)(2,1)}, u32[]{:S(2)}) %copy-start.1) | copy-done | bytes 786456
  4.9 0.0 copy-start.2
  4.9 0.9 %copy-done.2 = bf16[128,512]{1,0:T(8,128)(2,1)S(1)} copy-done((bf16[128,512]{1,0:T(8,128)(2,1)S(1)}, bf16[128,512]{1,0:T(8,128)(2,1)}, u32[]{:S(2)}) %copy-start.2) | copy-done | bytes 131096
  5.9 61.1 %contrast.1 = (bf16[128,512]{1,0:T(8,128)(2,1)S(1)}, f32[128,512]{1,0:T(8,128)S(1)}) custom-call(f32[1]{0:T(128)S(6)} %copy.8.nef_ref, f32[1]{0:T(128)S(6)} %copy.9.bias_ref, bf16[128,512]{1,0:T(8,128)(2,1)S(1)} %copy-done.2, bf16[128,3072]{1,0:T(8,128)(2,1)S(1)} %copy-done.1, bf16[3072,512]{1,0:T(8,128)(2,1)S(1)} %copy-done), custom_call_target="tpu_custom_call" | custom-call | tf_op jit(solution)/shard_map/contrast/pallas_call | solution.py:216
  67.0 2.3 %fusion = f32[128,3072]{1,0:T(8,128)} fusion(bf16[128,512]{1,0:T(8,128)(2,1)S(1)} %get-tuple-element.4, bf16[3072,512]{1,0:T(8,128)(2,1)S(1)} %copy-done), kind=kOutput, calls=%fused_computation | convolution fusion | flops 402653184 | bytes 4849664 | tf_op jit(solution)/shard_map/dot_general | solution.py:244
  69.2 0.7 %copy.10 = f32[128,512]{1,0:T(8,128)} copy(f32[128,512]{1,0:T(8,128)S(1)} %get-tuple-element.9) | data formatting | bytes 524288
Async XLA Ops:
  1.9 1.9 %copy-start = (bf16[3072,512]{1,0:T(8,128)(2,1)S(1)}, bf16[3072,512]{1,0:T(8,128)(2,1)}, u32[]{:S(2)}) copy-start(bf16[3072,512]{1,0:T(8,128)(2,1)} %head_hbm.1) | copy-start | bytes 9437188
  3.8 1.1 %copy-start.1 = (bf16[128,3072]{1,0:T(8,128)(2,1)S(1)}, bf16[128,3072]{1,0:T(8,128)(2,1)}, u32[]{:S(2)}) copy-start(bf16[128,3072]{1,0:T(8,128)(2,1)} %feat_hbm.1) | copy-start | bytes 2359300
  4.9 0.9 %copy-start.2 = (bf16[128,512]{1,0:T(8,128)(2,1)S(1)}, bf16[128,512]{1,0:T(8,128)(2,1)}, u32[]{:S(2)}) copy-start(bf16[128,512]{1,0:T(8,128)(2,1)} %txt_ref.1) | copy-start | bytes 393220

commit v2 on v1

v2 whole, which is shorter than its diff:
```python
import functools

import jax
import jax.numpy as jnp
from jax import lax
from jax.experimental import pallas as pl
from jax.experimental.pallas import tpu as pltpu
from jax.sharding import PartitionSpec as P

EPS = 1e-06
MESH = pl.DeviceIdType.MESH
N_Y = 8
N_BLK = 64
ROWS = 128
PARTS = 2
PART = 64
EMB = 512
WIDTH = 3072
K_CHUNKS = 4
LAST = (((1,), (1,)), ((), ()))

NEAR = {7: 0, 1: 1, 6: 2, 2: 3, 5: 4, 3: 5, 4: 6, 0: 7}
FAR = {0: 8, 4: 9, 7: 10, 1: 11, 6: 12, 2: 13, 5: 14, 3: 15}


def rows_of(place, part=None):
    if part is None:
        return pl.ds(place * ROWS, ROWS)
    return pl.ds(place * ROWS + part * PART, PART)


def kernel(
    nef_ref, bias_ref, txt_hbm, feat_hbm, head_hbm, dfeat_ref, dtext_ref,
    feat, head, txt_ref, txts, imgs, img_unit, img_acc, txt_acc,
    swap_out, swap_in, txt_out, txt_in, load_sem, send_sem, recv_sem,
):
    group = lax.axis_index("group")
    blk = lax.axis_index("blk")
    y, xh = group // 2, lax.rem(group, 2)
    up = {"group": lax.rem(y + 1, N_Y) * 2 + xh, "blk": blk}
    down = {"group": lax.rem(y + N_Y - 1, N_Y) * 2 + xh, "blk": blk}
    across = {"group": y * 2 + (1 - xh), "blk": blk}
    flip_next = jnp.where(blk == N_BLK - 1, 1 - xh, xh)
    flip_prev = jnp.where(blk == 0, 1 - xh, xh)
    after = {"group": y * 2 + flip_next, "blk": lax.rem(blk + 1, N_BLK)}
    before = {"group": y * 2 + flip_prev, "blk": lax.rem(blk + N_BLK - 1, N_BLK)}

    barrier = pltpu.get_barrier_semaphore()
    for peer in (up, down, across, after, before):
        pl.semaphore_signal(barrier, inc=1, device_id=peer, device_id_type=MESH)

    text_load = pltpu.make_async_copy(txt_hbm, txt_ref, load_sem.at[2 * K_CHUNKS])
    text_load.start()
    depth = WIDTH // K_CHUNKS
    loads = []
    for k in range(K_CHUNKS):
        span = pl.ds(k * depth, depth)
        pair = (
            pltpu.make_async_copy(feat_hbm.at[:, span], feat.at[:, span], load_sem.at[2 * k]),
            pltpu.make_async_copy(head_hbm.at[span], head.at[span], load_sem.at[2 * k + 1]),
        )
        for copy in pair:
            copy.start()
        loads.append(pair)

    copies = []

    def send(src, dst, peer):
        i = len(copies)
        copy = pltpu.make_async_remote_copy(
            src_ref=src, dst_ref=dst, send_sem=send_sem.at[i], recv_sem=recv_sem.at[i],
            device_id=peer, device_id_type=MESH,
        )
        copy.start()
        copies.append(copy)
        return copy

    def ring_hop(buf, places, moved, step):
        for part in range(PARTS):
            for way, peer in ((-1, up), (1, down)):
                src = (way * step) % N_Y
                dst = (way * (step + 1)) % N_Y
                if step == 3 and (part < PARTS // 2) != (way == -1):
                    continue
                if step:
                    moved[src, part].wait_recv()
                moved[dst, part] = send(
                    buf.at[rows_of(places[src], part)], buf.at[rows_of(places[dst], part)], peer
                )
        if step == 3:
            for part in range(PARTS):
                moved[5 if part >= PARTS // 2 else 3, part].wait_recv()

    def ring_end(moved):
        for part in range(PARTS):
            moved[4, part].wait_recv()

    def hand_on(slot):
        handed[slot] = send(txts.at[rows_of(NEAR[slot])], txts.at[rows_of(FAR[slot])], after)

    txt_moved, img_moved, swp_moved, handed = {}, {}, {}, {}

    text_load.wait()
    words = txt_ref[...].astype(jnp.float32)
    txt_inv = lax.rsqrt(jnp.sum(words * words, axis=-1, keepdims=True) + EPS)
    txts[rows_of(NEAR[0])] = (words * txt_inv).astype(jnp.bfloat16)

    scale = jnp.exp(jnp.full((1, 1), nef_ref[0], jnp.float32))
    half_scale = 0.5 * scale
    half_bias = 0.5 * bias_ref[0]

    pl.semaphore_wait(barrier, 5)
    ring_hop(txts, NEAR, txt_moved, 0)
    hand_on(0)

    projected = jnp.zeros((ROWS, EMB), jnp.float32)
    for k in range(K_CHUNKS):
        span = pl.ds(k * depth, depth)
        for copy in loads[k]:
            copy.wait()
        projected += jnp.dot(feat[:, span], head[span], preferred_element_type=jnp.float32)
    img_inv = lax.rsqrt(jnp.sum(projected * projected, axis=-1, keepdims=True) + EPS)
    unit = projected * img_inv
    img_unit[...] = unit
    imgs[rows_of(NEAR[0])] = unit.astype(jnp.bfloat16)

    swapped = send(imgs.at[rows_of(NEAR[0])], imgs.at[rows_of(FAR[0])], across)
    ring_hop(imgs, NEAR, img_moved, 0)

    def terms(left, buf, place, pieces, own=False):
        right = buf[pl.ds(place * ROWS, pieces * ROWS)]
        dots = lax.dot_general(left, right, LAST, preferred_element_type=jnp.float32)
        weight = 0.5 * jnp.tanh(half_scale * dots + half_bias) + 0.5
        if own:
            row = lax.broadcasted_iota(jnp.int32, weight.shape, 0)
            col = lax.broadcasted_iota(jnp.int32, weight.shape, 1)
            weight = jnp.where(col == row + (pieces - 1) * ROWS, weight - 1.0, weight)
        return jnp.dot(weight.astype(jnp.bfloat16), right, preferred_element_type=jnp.float32)

    def both_imgs():
        return imgs[pl.ds(NEAR[0] * ROWS, 2 * ROWS)]

    def both_txts():
        return txts[pl.ds(NEAR[0] * ROWS, 2 * ROWS)]

    def add_img(place, own=False):
        img_acc[...] += terms(both_imgs(), txts, place, 2, own)

    def add_txt(place, own=False):
        txt_acc[...] += terms(both_txts(), imgs, place, 2, own)

    ring_hop(txts, NEAR, txt_moved, 1)
    hand_on(7)
    hand_on(1)
    ring_hop(imgs, NEAR, img_moved, 1)
    ring_hop(txts, NEAR, txt_moved, 2)
    hand_on(6)
    hand_on(2)
    swapped.wait_recv()
    ring_hop(imgs, FAR, swp_moved, 0)
    img_acc[...] = terms(both_imgs(), txts, 0, 2)
    ring_hop(txts, NEAR, txt_moved, 3)
    hand_on(5)
    hand_on(3)
    ring_hop(imgs, NEAR, img_moved, 2)
    add_img(2)
    ring_end(txt_moved)
    hand_on(4)
    ring_hop(imgs, FAR, swp_moved, 1)
    add_img(4)
    add_img(6, own=True)
    ring_hop(imgs, NEAR, img_moved, 3)
    for a, b in ((7, 1), (6, 2), (5, 3), (0, 4)):
        handed[a].wait_recv()
        handed[b].wait_recv()
        add_img(min(FAR[a], FAR[b]))
    swap_out[...] = img_acc[ROWS:].astype(jnp.bfloat16)
    returned = send(swap_out, swap_in, across)

    ring_hop(imgs, FAR, swp_moved, 2)
    txt_acc[...] = terms(both_txts(), imgs, 0, 2)
    add_txt(2)
    add_txt(4)
    ring_hop(imgs, FAR, swp_moved, 3)
    ring_end(img_moved)
    add_txt(6, own=True)
    add_txt(10)
    add_txt(12)
    add_txt(14)
    ring_end(swp_moved)
    add_txt(8)
    txt_out[...] = txt_acc[ROWS:].astype(jnp.bfloat16)
    given = send(txt_out, txt_in, before)

    def back(grad, unit_rows, inverse):
        return (grad - unit_rows * jnp.sum(unit_rows * grad, axis=-1, keepdims=True)) * inverse

    returned.wait_recv()
    grad = scale * (img_acc[:ROWS] + swap_in[...].astype(jnp.float32))
    img_back = back(grad, img_unit[...], img_inv).astype(jnp.bfloat16)
    for k in range(K_CHUNKS):
        span = pl.ds(k * depth, depth)
        dfeat_ref[:, span] = lax.dot_general(img_back, head[span], LAST, preferred_element_type=jnp.float32)
    given.wait_recv()
    grad = scale * (txt_acc[:ROWS] + txt_in[...].astype(jnp.float32))
    words = txt_ref[...].astype(jnp.float32)
    dtext_ref[...] = back(grad, words * txt_inv, txt_inv)

    for copy in copies:
        copy.wait_send()


N_COPIES = 3 * 7 * PARTS + 8 + 3


def body(img_feat, head_weight, text_emb, natural_exponent_factor, bias):
    smem = pl.BlockSpec(memory_space=pltpu.SMEM)
    vmem = pl.BlockSpec(memory_space=pltpu.VMEM)
    hbm = pl.BlockSpec(memory_space=pl.ANY)
    return pl.pallas_call(
        kernel,
        out_shape=(
            jax.ShapeDtypeStruct((ROWS, WIDTH), jnp.float32),
            jax.ShapeDtypeStruct((ROWS, EMB), jnp.float32),
        ),
        in_specs=[smem, smem, hbm, hbm, hbm],
        out_specs=(vmem, vmem),
        scratch_shapes=[
            pltpu.VMEM((ROWS, WIDTH), jnp.bfloat16),
            pltpu.VMEM((WIDTH, EMB), jnp.bfloat16),
            pltpu.VMEM((ROWS, EMB), jnp.bfloat16),
            pltpu.VMEM((16 * ROWS, EMB), jnp.bfloat16),
            pltpu.VMEM((16 * ROWS, EMB), jnp.bfloat16),
            pltpu.VMEM((ROWS, EMB), jnp.float32),
            pltpu.VMEM((2 * ROWS, EMB), jnp.float32),
            pltpu.VMEM((2 * ROWS, EMB), jnp.float32),
            pltpu.VMEM((ROWS, EMB), jnp.bfloat16),
            pltpu.VMEM((ROWS, EMB), jnp.bfloat16),
            pltpu.VMEM((ROWS, EMB), jnp.bfloat16),
            pltpu.VMEM((ROWS, EMB), jnp.bfloat16),
            pltpu.SemaphoreType.DMA((2 * K_CHUNKS + 1,)),
            pltpu.SemaphoreType.DMA((N_COPIES,)),
            pltpu.SemaphoreType.DMA((N_COPIES,)),
        ],
        compiler_params=pltpu.CompilerParams(collective_id=0, has_side_effects=True, vmem_limit_bytes=67043328),
        name="contrast",
    )(natural_exponent_factor, bias, text_emb, img_feat, head_weight)


def solution(mesh):
    return jax.shard_map(
        body,
        mesh=mesh,
        in_specs=(P(("blk", "group"), None), P(), P(("blk", "group"), None), P(), P()),
        out_specs=(P(("blk", "group"), None), P(("blk", "group"), None)),
        check_vma=False,
    )
```

time: 70.2 us -> 65.2 us (0.929)
  the two profiles are of different devices: /device:TPU:2 before, /device:TPU:16 now
where the time goes in v2:
time: 65.2 us; the launch traced here: 65 us
  Pallas kernels  59.7 us (92%)
  local copies, waits for them, and re-layouts  3.45 us (5%)
  between operations  1.94 us (3%)
    pallas_call x1, Pallas kernels, body(): pl.pallas_call(kernel, out_shape=(jax.ShapeDtypeStruct((ROWS, WIDTH), jnp...  59.7 us
    unnamed x4, local copies, waits for them, and re-layouts  3.45 us

profile of v2, /device:TPU:16, one launch (start us, length us, event | category | flops | bytes accessed | tf_op | source)
XLA Modules:
  0.0 65.0 jit_solution(13478725300727121919)
XLA Ops:
  1.9 59.7 %contrast.1 = (f32[128,3072]{1,0:T(8,128)}, f32[128,512]{1,0:T(8,128)}) custom-call(f32[1]{0:T(128)S(6)} %copy.9.nef_ref, f32[1]{0:T(128)S(6)} %copy.10.bias_ref, bf16[128,512]{1,0:T(8,128)(2,1)} %txt_hbm.1, bf16[128,3072]{1,0:T(8,128)(2,1)} %feat_hbm.1, bf16[3072,512]{1,0:T(8,128)(2,1)} %head_hbm.1), custom_call_target="tpu_custom_call" | custom-call | tf_op jit(solution)/shard_map/contrast/pallas_call | solution.py:220
  61.6 0.0 copy-start
  61.6 2.7 %copy.11 = f32[128,3072]{1,0:T(8,128)} copy(f32[128,3072]{1,0:T(8,128)} %get-tuple-element.4) | data formatting | bytes 3145728
  64.3 0.0 copy-done
  64.3 0.7 %copy.12 = f32[128,512]{1,0:T(8,128)} copy(f32[128,512]{1,0:T(8,128)S(1)} %copy-done) | data formatting | bytes 524288
Async XLA Ops:
  61.6 2.8 %copy-start = (f32[128,512]{1,0:T(8,128)S(1)}, f32[128,512]{1,0:T(8,128)}, u32[]{:S(2)}) copy-start(f32[128,512]{1,0:T(8,128)} %get-tuple-element.5) | copy-start | bytes 786436

commit v3 on v2

--- a/solution.py
+++ b/solution.py
@@ -170,18 +170,25 @@
     add_img(4)
     add_img(6, own=True)
     ring_hop(imgs, NEAR, img_moved, 3)
-    for a, b in ((7, 1), (6, 2), (5, 3), (0, 4)):
-        handed[a].wait_recv()
-        handed[b].wait_recv()
-        add_img(min(FAR[a], FAR[b]))
+    ring_hop(imgs, FAR, swp_moved, 2)
+    handed[7].wait_recv()
+    handed[1].wait_recv()
+    add_img(10)
+    handed[6].wait_recv()
+    handed[2].wait_recv()
+    add_img(12)
+    handed[5].wait_recv()
+    handed[3].wait_recv()
+    add_img(14)
+    handed[0].wait_recv()
+    handed[4].wait_recv()
+    add_img(8)
     swap_out[...] = img_acc[ROWS:].astype(jnp.bfloat16)
     returned = send(swap_out, swap_in, across)
-
-    ring_hop(imgs, FAR, swp_moved, 2)
+    ring_hop(imgs, FAR, swp_moved, 3)
     txt_acc[...] = terms(both_txts(), imgs, 0, 2)
     add_txt(2)
     add_txt(4)
-    ring_hop(imgs, FAR, swp_moved, 3)
     ring_end(img_moved)
     add_txt(6, own=True)
     add_txt(10)

time: 65.2 us -> 61.8 us (0.948)
  the two profiles are of different devices: /device:TPU:16 before, /device:TPU:32 now
where the time goes in v3:
time: 61.8 us; the launch traced here: 61.6 us
  Pallas kernels  56.2 us (91%)
  local copies, waits for them, and re-layouts  3.45 us (6%)
  between operations  1.94 us (3%)
    pallas_call x1, Pallas kernels, body(): pl.pallas_call(kernel, out_shape=(jax.ShapeDtypeStruct((ROWS, WIDTH), jnp...  56.2 us
    unnamed x4, local copies, waits for them, and re-layouts  3.45 us

profile of v3, /device:TPU:32, one launch (start us, length us, event | category | flops | bytes accessed | tf_op | source)
XLA Modules:
  0.0 61.6 jit_solution(10251693566395517204)
XLA Ops:
  1.9 56.2 %contrast.1 = (f32[128,3072]{1,0:T(8,128)}, f32[128,512]{1,0:T(8,128)}) custom-call(f32[1]{0:T(128)S(6)} %copy.9.nef_ref, f32[1]{0:T(128)S(6)} %copy.10.bias_ref, bf16[128,512]{1,0:T(8,128)(2,1)} %txt_hbm.1, bf16[128,3072]{1,0:T(8,128)(2,1)} %feat_hbm.1, bf16[3072,512]{1,0:T(8,128)(2,1)} %head_hbm.1), custom_call_target="tpu_custom_call" | custom-call | tf_op jit(solution)/shard_map/contrast/pallas_call | solution.py:227
  58.1 0.0 copy-start
  58.2 2.7 %copy.11 = f32[128,3072]{1,0:T(8,128)} copy(f32[128,3072]{1,0:T(8,128)} %get-tuple-element.4) | data formatting | bytes 3145728
  60.9 0.0 copy-done
  60.9 0.7 %copy.12 = f32[128,512]{1,0:T(8,128)} copy(f32[128,512]{1,0:T(8,128)S(1)} %copy-done) | data formatting | bytes 524288
Async XLA Ops:
  58.1 2.8 %copy-start = (f32[128,512]{1,0:T(8,128)S(1)}, f32[128,512]{1,0:T(8,128)}, u32[]{:S(2)}) copy-start(f32[128,512]{1,0:T(8,128)} %get-tuple-element.5) | copy-start | bytes 786436

commit v4 on v3

--- a/solution.py
+++ b/solution.py
@@ -30,9 +30,9 @@
 
 
 def kernel(
-    nef_ref, bias_ref, txt_hbm, feat_hbm, head_hbm, dfeat_ref, dtext_ref,
-    feat, head, txt_ref, txts, imgs, img_unit, img_acc, txt_acc,
-    swap_out, swap_in, txt_out, txt_in, load_sem, send_sem, recv_sem,
+    nef_ref, bias_ref, txt_hbm, feat_hbm, head_hbm, dfeat_hbm, dtext_ref,
+    feat, head, txt_ref, dfeat, txts, imgs, img_unit, img_acc, txt_acc,
+    swap_out, swap_in, txt_out, txt_in, load_sem, out_sem, send_sem, recv_sem,
 ):
     group = lax.axis_index("group")
     blk = lax.axis_index("blk")
@@ -82,7 +82,7 @@
                 dst = (way * (step + 1)) % N_Y
                 if step == 3 and (part < PARTS // 2) != (way == -1):
                     continue
-                if step:
+                if step or ((0, part) in moved and way == -1):
                     moved[src, part].wait_recv()
                 moved[dst, part] = send(
                     buf.at[rows_of(places[src], part)], buf.at[rows_of(places[dst], part)], peer
@@ -124,7 +124,10 @@
     img_unit[...] = unit
     imgs[rows_of(NEAR[0])] = unit.astype(jnp.bfloat16)
 
-    swapped = send(imgs.at[rows_of(NEAR[0])], imgs.at[rows_of(FAR[0])], across)
+    for part in range(PARTS):
+        swp_moved[0, part] = send(
+            imgs.at[rows_of(NEAR[0], part)], imgs.at[rows_of(FAR[0], part)], across
+        )
     ring_hop(imgs, NEAR, img_moved, 0)
 
     def terms(left, buf, place, pieces, own=False):
@@ -156,7 +159,6 @@
     ring_hop(txts, NEAR, txt_moved, 2)
     hand_on(6)
     hand_on(2)
-    swapped.wait_recv()
     ring_hop(imgs, FAR, swp_moved, 0)
     img_acc[...] = terms(both_imgs(), txts, 0, 2)
     ring_hop(txts, NEAR, txt_moved, 3)
@@ -205,19 +207,24 @@
     returned.wait_recv()
     grad = scale * (img_acc[:ROWS] + swap_in[...].astype(jnp.float32))
     img_back = back(grad, img_unit[...], img_inv).astype(jnp.bfloat16)
+    stores = []
     for k in range(K_CHUNKS):
         span = pl.ds(k * depth, depth)
-        dfeat_ref[:, span] = lax.dot_general(img_back, head[span], LAST, preferred_element_type=jnp.float32)
+        dfeat[:, span] = lax.dot_general(img_back, head[span], LAST, preferred_element_type=jnp.float32)
+        stores.append(pltpu.make_async_copy(dfeat.at[:, span], dfeat_hbm.at[:, span], out_sem.at[k]))
+        stores[k].start()
     given.wait_recv()
     grad = scale * (txt_acc[:ROWS] + txt_in[...].astype(jnp.float32))
     words = txt_ref[...].astype(jnp.float32)
     dtext_ref[...] = back(grad, words * txt_inv, txt_inv)
 
+    for copy in stores:
+        copy.wait()
     for copy in copies:
         copy.wait_send()
 
 
-N_COPIES = 3 * 7 * PARTS + 8 + 3
+N_COPIES = 3 * 7 * PARTS + 8 + 2 + PARTS
 
 
 def body(img_feat, head_weight, text_emb, natural_exponent_factor, bias):
@@ -231,11 +238,12 @@
             jax.ShapeDtypeStruct((ROWS, EMB), jnp.float32),
         ),
         in_specs=[smem, smem, hbm, hbm, hbm],
-        out_specs=(vmem, vmem),
+        out_specs=(hbm, vmem),
         scratch_shapes=[
             pltpu.VMEM((ROWS, WIDTH), jnp.bfloat16),
             pltpu.VMEM((WIDTH, EMB), jnp.bfloat16),
             pltpu.VMEM((ROWS, EMB), jnp.bfloat16),
+            pltpu.VMEM((ROWS, WIDTH), jnp.float32),
             pltpu.VMEM((16 * ROWS, EMB), jnp.bfloat16),
             pltpu.VMEM((16 * ROWS, EMB), jnp.bfloat16),
             pltpu.VMEM((ROWS, EMB), jnp.float32),
@@ -246,6 +254,7 @@
             pltpu.VMEM((ROWS, EMB), jnp.bfloat16),
             pltpu.VMEM((ROWS, EMB), jnp.bfloat16),
             pltpu.SemaphoreType.DMA((2 * K_CHUNKS + 1,)),
+            pltpu.SemaphoreType.DMA((K_CHUNKS,)),
             pltpu.SemaphoreType.DMA((N_COPIES,)),
             pltpu.SemaphoreType.DMA((N_COPIES,)),
         ],

time: 61.8 us -> 61.8 us (level)
  the two profiles are of different devices: /device:TPU:32 before, /device:TPU:2 now
where the time goes in v4:
time: 61.8 us; the launch traced here: 61.6 us
  Pallas kernels  56.2 us (91%)
  local copies, waits for them, and re-layouts  3.45 us (6%)
  between operations  1.94 us (3%)
    pallas_call x1, Pallas kernels, body(): pl.pallas_call(kernel, out_shape=(jax.ShapeDtypeStruct((ROWS, WIDTH), jnp...  56.2 us
    unnamed x4, local copies, waits for them, and re-layouts  3.45 us

profile of v4, /device:TPU:2, one launch (start us, length us, event | category | flops | bytes accessed | tf_op | source)
XLA Modules:
  0.0 61.6 jit_solution(6468941012027229101)
XLA Ops:
  1.9 56.2 %contrast.1 = (f32[128,3072]{1,0:T(8,128)}, f32[128,512]{1,0:T(8,128)}) custom-call(f32[1]{0:T(128)S(6)} %copy.9.nef_ref, f32[1]{0:T(128)S(6)} %copy.10.bias_ref, bf16[128,512]{1,0:T(8,128)(2,1)} %txt_hbm.1, bf16[128,3072]{1,0:T(8,128)(2,1)} %feat_hbm.1, bf16[3072,512]{1,0:T(8,128)(2,1)} %head_hbm.1), custom_call_target="tpu_custom_call" | custom-call | tf_op jit(solution)/shard_map/contrast/pallas_call | solution.py:234
  58.1 0.0 copy-start
  58.1 2.7 %copy.11 = f32[128,3072]{1,0:T(8,128)} copy(f32[128,3072]{1,0:T(8,128)} %get-tuple-element.4) | data formatting | bytes 3145728
  60.9 0.0 copy-done
  60.9 0.7 %copy.12 = f32[128,512]{1,0:T(8,128)} copy(f32[128,512]{1,0:T(8,128)S(1)} %copy-done) | data formatting | bytes 524288
Async XLA Ops:
  58.1 2.8 %copy-start = (f32[128,512]{1,0:T(8,128)S(1)}, f32[128,512]{1,0:T(8,128)}, u32[]{:S(2)}) copy-start(f32[128,512]{1,0:T(8,128)} %get-tuple-element.5) | copy-start | bytes 786436

commit v5 on v3

--- a/solution.py
+++ b/solution.py
@@ -82,7 +82,7 @@
                 dst = (way * (step + 1)) % N_Y
                 if step == 3 and (part < PARTS // 2) != (way == -1):
                     continue
-                if step:
+                if step or ((0, part) in moved and way == -1):
                     moved[src, part].wait_recv()
                 moved[dst, part] = send(
                     buf.at[rows_of(places[src], part)], buf.at[rows_of(places[dst], part)], peer
@@ -124,7 +124,10 @@
     img_unit[...] = unit
     imgs[rows_of(NEAR[0])] = unit.astype(jnp.bfloat16)
 
-    swapped = send(imgs.at[rows_of(NEAR[0])], imgs.at[rows_of(FAR[0])], across)
+    for part in range(PARTS):
+        swp_moved[0, part] = send(
+            imgs.at[rows_of(NEAR[0], part)], imgs.at[rows_of(FAR[0], part)], across
+        )
     ring_hop(imgs, NEAR, img_moved, 0)
 
     def terms(left, buf, place, pieces, own=False):
@@ -156,7 +159,6 @@
     ring_hop(txts, NEAR, txt_moved, 2)
     hand_on(6)
     hand_on(2)
-    swapped.wait_recv()
     ring_hop(imgs, FAR, swp_moved, 0)
     img_acc[...] = terms(both_imgs(), txts, 0, 2)
     ring_hop(txts, NEAR, txt_moved, 3)
@@ -217,7 +219,7 @@
         copy.wait_send()
 
 
-N_COPIES = 3 * 7 * PARTS + 8 + 3
+N_COPIES = 3 * 7 * PARTS + 8 + 2 + PARTS
 
 
 def body(img_feat, head_weight, text_emb, natural_exponent_factor, bias):
@@ -249,7 +251,7 @@
             pltpu.SemaphoreType.DMA((N_COPIES,)),
             pltpu.SemaphoreType.DMA((N_COPIES,)),
         ],
-        compiler_params=pltpu.CompilerParams(collective_id=0, has_side_effects=True, vmem_limit_bytes=67043328),
+        compiler_params=pltpu.CompilerParams(collective_id=0, has_side_effects=True, vmem_limit_bytes=50*2**20),
         name="contrast",
     )(natural_exponent_factor, bias, text_emb, img_feat, head_weight)
 

time: 61.8 us -> 61.4 us (level)
  Pallas kernels: 56.2 us -> 55.4 us
    pallas_call x1, Pallas kernels: 56.2 us -> 55.4 us  [body(): pl.pallas_call(kernel, out_shape=(jax.ShapeDtypeStruct((ROWS, WIDTH), jnp...]
    unnamed x4 -> x6, local copies, waits for them, and re-layouts: 3.45 us -> 3.88 us
where the time goes in v5:
time: 61.4 us; the launch traced here: 61.2 us
  Pallas kernels  55.4 us (90%)
  local copies, waits for them, and re-layouts  3.88 us (6%)
  between operations  1.94 us (3%)
    pallas_call x1, Pallas kernels, body(): pl.pallas_call(kernel, out_shape=(jax.ShapeDtypeStruct((ROWS, WIDTH), jnp...  55.4 us
    unnamed x6, local copies, waits for them, and re-layouts  3.88 us

profile of v5, /device:TPU:32, one launch (start us, length us, event | category | flops | bytes accessed | tf_op | source)
XLA Modules:
  0.0 61.2 jit_solution(8239135604851441735)
XLA Ops:
  1.9 0.0 copy-start
  1.9 1.1 %copy-done = bf16[128,3072]{1,0:T(8,128)(2,1)S(1)} copy-done((bf16[128,3072]{1,0:T(8,128)(2,1)S(1)}, bf16[128,3072]{1,0:T(8,128)(2,1)}, u32[]{:S(2)}) %copy-start) | copy-done | bytes 786456
  3.1 0.0 copy-start.1
  3.1 0.9 %copy-done.1 = bf16[128,512]{1,0:T(8,128)(2,1)S(1)} copy-done((bf16[128,512]{1,0:T(8,128)(2,1)S(1)}, bf16[128,512]{1,0:T(8,128)(2,1)}, u32[]{:S(2)}) %copy-start.1) | copy-done | bytes 131096
  4.0 55.4 %contrast.1 = (f32[128,3072]{1,0:T(8,128)S(1)}, f32[128,512]{1,0:T(8,128)S(1)}) custom-call(f32[1]{0:T(128)S(6)} %copy.9.nef_ref, f32[1]{0:T(128)S(6)} %copy.10.bias_ref, bf16[128,512]{1,0:T(8,128)(2,1)S(1)} %copy-done.1, bf16[128,3072]{1,0:T(8,128)(2,1)S(1)} %copy-done, bf16[3072,512]{1,0:T(8,128)(2,1)} %head_hbm.1), custom_call_target="tpu_custom_call" | custom-call | tf_op jit(solution)/shard_map/contrast/pallas_call | solution.py:229
  59.3 1.1 %copy.11 = f32[128,3072]{1,0:T(8,128)} copy(f32[128,3072]{1,0:T(8,128)S(1)} %get-tuple-element.4) | data formatting | bytes 3145728
  60.5 0.7 %copy.12 = f32[128,512]{1,0:T(8,128)} copy(f32[128,512]{1,0:T(8,128)S(1)} %get-tuple-element.5) | data formatting | bytes 524288
Async XLA Ops:
  1.9 1.1 %copy-start = (bf16[128,3072]{1,0:T(8,128)(2,1)S(1)}, bf16[128,3072]{1,0:T(8,128)(2,1)}, u32[]{:S(2)}) copy-start(bf16[128,3072]{1,0:T(8,128)(2,1)} %feat_hbm.1) | copy-start | bytes 2359300
  3.1 0.9 %copy-start.1 = (bf16[128,512]{1,0:T(8,128)(2,1)S(1)}, bf16[128,512]{1,0:T(8,128)(2,1)}, u32[]{:S(2)}) copy-start(bf16[128,512]{1,0:T(8,128)(2,1)} %txt_hbm.1) | copy-start | bytes 393220
